TPU v7x, 256 devices: a whole 4x4x8 slice. The times are simulated.
256 devices in a mesh: task: 8 (over x_hi, y), mp: 32 (over x_lo, z, core).
Axes of the slice: x: 4 (x_hi: 2, x_lo: 2; x = x_hi * 2 + x_lo), y: 4, z: 8, core: 2. Of those that a mesh axis runs over, the one named last changes fastest.
Arguments:
- hidden: bfloat16 [8, 2048, 8192], P('task', 'mp'), may hold values from -6 to 6
- gain: float32 [8192], replicated, may hold values from 0.25 to 1.75
- tau: bfloat16 [8, 8192, 1024], P('task', 'mp'), may hold values from -0.0625 to 0.0625
- coeff: float32 [8, 8192, 1024], P('task', 'mp'), may hold values from 0.1 to 1
- counts: int32 [8], P('task'), may hold values from 683 to 2048, as said below
- positions: int32 [8, 2048], P('task', 'mp'), may hold values from 0 to 2047
Outputs:
- grad_coeff: float32 [8, 8192, 1024], P('task', 'mp')
- loss: float32 [], replicated
Inputs may be any that keep to these rules, and one draw needn't show every extreme that they name: `counts`: counts lie between a third of 2048 and 2048; some task has exactly 2048 in every draw. Rows at or past a task's count are not live.
All inputs are finite; a program needn't handle non-finite values.
Results may differ from a plain program's by a relative error of at most 0.0044.
The roundings to bfloat16 on the way count: a program that leaves them out, or rounds other values in their place, can miss the bound.
Values may be sent and summed in bfloat16 or wider, within the bound.
A program may use at most 64 MiB of HBM per device.

v0:
```python
import jax
import jax.numpy as jnp
from jax import lax
from jax.sharding import Mesh
from jax.sharding import PartitionSpec as P

HEAD = 128
MP = ("mp_0", "mp_1", "mp_2")
TASK = ("task_0", "task_1")
TASK_MP = ("task_0", "task_1", "mp_0", "mp_1", "mp_2")


def cut_along(value, dim, length):
    before, after = (value.shape[:dim], value.shape[dim + 1 :])
    return jnp.moveaxis(value.reshape(*before, length, -1, *after), dim, 0)


def scatter_pairs(value, chips, core, dim):
    sizes = (lax.axis_size(chips), lax.axis_size(core))
    tiles = cut_along(value, dim, sizes[0] * sizes[1])
    inside = tiles.shape[1:]
    tiles = tiles.reshape(*sizes, *inside).swapaxes(0, 1).reshape(-1, *inside)
    tiles = lax.psum_scatter(tiles, core, scatter_dimension=0, tiled=True)
    return lax.psum_scatter(tiles, chips, scatter_dimension=0, tiled=True)[0]


def by_axis(value, axes):
    for axis in axes:
        value = lax.psum(value, axis)
    return value


def rotary_tables(positions, head):
    index = jnp.arange(head // 2).astype(jnp.float32)
    freq = jnp.exp(-jnp.log(jnp.float32(1000000.0)) * 2.0 * index / head)
    angle = positions.astype(jnp.float32)[:, None] * freq[None, :]
    return (jnp.cos(angle), jnp.sin(angle))


def rotate(values, cosine, sine, sign, head):
    count = values.shape[0]
    width = values.shape[1]
    shaped = values.reshape(count, width // head, 2, head // 2)
    first = shaped[:, :, 0, :]
    second = shaped[:, :, 1, :]
    cosine = cosine[:, None, :]
    sine = sine[:, None, :] * sign
    out_first = first * cosine - second * sine
    out_second = second * cosine + first * sine
    return jnp.stack([out_first, out_second], axis=2).reshape(count, width)


def local(hidden, gain, tau, coeff, counts, positions):
    rows = hidden[0].astype(jnp.float32)
    width = rows.shape[1]
    keys = tau.shape[2]
    rows_local = rows.shape[0]
    inverse = 1.0 / jnp.sqrt(jnp.mean(rows * rows, axis=1, keepdims=True) + 1e-06)
    normed = (rows * inverse * gain[None, :]).astype(jnp.bfloat16)
    columns = lax.all_to_all(normed, MP, split_axis=1, concat_axis=0, tiled=True)
    tau_local = tau[0].astype(jnp.float32)
    mixed = lax.psum(coeff[0] * tau_local, TASK)
    merged = mixed.astype(jnp.bfloat16)
    teacher = tau[0]
    block = columns
    gap = scatter_pairs(
        jnp.dot(block, merged, preferred_element_type=jnp.float32)
        - jnp.dot(block, teacher, preferred_element_type=jnp.float32),
        ("mp_0", "mp_1"),
        "mp_2",
        0,
    )
    first_row = lax.axis_index(MP) * rows_local
    cosine, sine = rotary_tables(positions[0], HEAD)
    err = rotate(gap, cosine, sine, 1.0, HEAD)
    row_ids = first_row + jnp.arange(rows_local)
    live = (row_ids < counts[0]).astype(jnp.float32)[:, None]
    scale = 1.0 / (counts[0].astype(jnp.float32) * keys)
    partial_loss = jnp.sum(live * err * err) * scale
    back = rotate(2.0 * scale * live * err, cosine, sine, -1.0, HEAD).astype(jnp.bfloat16)
    block = columns
    local_grad = lax.dot_general(
        block,
        lax.all_gather(back, MP, axis=0, tiled=True),
        (((0,), (0,)), ((), ())),
        preferred_element_type=jnp.float32,
    )
    wgrad = lax.psum(local_grad, TASK)
    loss = by_axis(partial_loss, TASK_MP)
    grad_coeff = width * keys * tau_local * wgrad
    return (grad_coeff[None, :, :], loss)


def solution(mesh):
    split = Mesh(mesh.devices.reshape(2, 4, 2, 8, 2), ("task_0", "task_1", "mp_0", "mp_1", "mp_2"))
    placed = (P(TASK, MP, None), P(), P(TASK, MP, None), P(TASK, MP, None), P(TASK), P(TASK, MP))
    return jax.shard_map(
        local, mesh=split, in_specs=placed, out_specs=(P(TASK, MP, None), P()), check_vma=False
    )
```

profile of v0, /device:TPU:32, one launch (start us, length us, event | category | flops | bytes accessed | tf_op | source)
XLA Modules:
  0.0 391.9 jit_solution(13827501548182623606)
XLA Ops:
  7.2 1.5 multiply_reduce_fusion
  8.7 1.5 copy.13
  10.6 1.6 copy.11
  12.1 9.7 %all-to-all-start = ((bf16[64,32,256]{2,0,1:T(8,128)(2,1)}), bf16[64,32,256]{2,0,1:T(8,128)(2,1)S(1)}, u32[]{:S(2)}, u32[]{:S(2)}) async-start(bf16[64,32,256]{2,0,1:T(8,128)(2,1)} %copy.11), calls=%async_computation | async-start | bytes 2097152 | tf_op jit(solution)/shard_map/all_to_all | solution.py:60
  21.8 1.4 convert_multiply_fusion
  23.2 81.8 %all-reduce.4 = bf16[256,1024]{1,0:T(8,128)(2,1)S(1)} all-reduce(f32[256,1024]{1,0:T(8,128)S(1)} %convert_multiply_fusion), channel_id=1, replica_groups=mesh['task_0'=2,'task_1'=4,'mp_0'=2,'mp_1'=8,'mp_2'=2] {'task_0','task_1'}, use_global_device_ids=true, to_apply=%region_1.0 | all-reduce | flops 262144 | bytes 1572864 | tf_op jit(solution)/shard_map/psum | solution.py:62
  105.0 1.3 fusion.9
  106.3 1.3 convolution_subtract_fusion
  107.6 4.1 %copy.12 = f32[16,2,64,1024]{3,2,0,1:T(8,128)} copy(f32[16,2,64,1024]{3,2,1,0:T(8,128)S(1)} %bitcast.36) | data formatting | bytes 16777216 | tf_op jit(solution)/shard_map/reshape;reshape | solution.py:22
  111.7 19.8 %reduce-scatter.3.cloned.1.call-done = f32[16,64,1024]{2,1,0:T(8,128)} async-done(((f32[32,64,1024]{2,1,0:T(8,128)}), f32[16,64,1024]{2,1,0:T(8,128)}) %reduce-scatter.3.cloned.1.call-update) | async-done | bytes 4194320 | tf_op jit(solution)/shard_map/reduce_scatter | solution.py:23
  132.6 81.7 %reduce-scatter.5.cloned.1.call-done = f32[1,64,1024]{2,1,0:T(8,128)} async-done(((f32[16,64,1024]{2,1,0:T(8,128)}), f32[1,64,1024]{2,1,0:T(8,128)}) %reduce-scatter.5.cloned.1.call-update) | async-done | bytes 262160 | tf_op jit(solution)/shard_map/reduce_scatter | solution.py:24
  214.2 1.3 reshape_squeeze.3
  216.2 1.8 fusion.4
  218.6 0.7 pad_maximum_fusion.1
  219.3 0.9 convert_element_type.62
  220.3 64.3 %all-gather.2.cloned.1.call-done = bf16[2048,1024]{1,0:T(8,128)(2,1)} async-done(((bf16[64,1024]{1,0:T(8,128)(2,1)}), bf16[2048,1024]{1,0:T(8,128)(2,1)}) %all-gather.2.cloned.1.call-update) | async-done | bytes 4194320 | tf_op jit(solution)/shard_map/all_gather | solution.py:84
  284.5 4.4 %fusion.8 = f32[256,1024]{1,0:T(8,128)} fusion(bf16[2048,256]{1,0:T(8,128)(2,1)S(1)} %bitcast.40, bf16[2048,1024]{1,0:T(8,128)(2,1)} %all-gather.2.cloned.1.call-done), kind=kOutput, calls=%fused_computation.30 | convolution fusion | flops 1073741824 | bytes 6291456 | tf_op jit(solution)/shard_map/dot_general | solution.py:82
  289.6 6.9 %psum.51 = f32[]{:T(128)} all-reduce(f32[]{:T(128)S(6)} %mul.221), channel_id=1, replica_groups=mesh['task_0'=2,'task_1'=4,'mp_0'=2,'mp_1'=8,'mp_2'=2] {'task_0'}, use_global_device_ids=true, to_apply=%region_6.0 | all-reduce | flops 1 | bytes 8 | tf_op jit(solution)/shard_map/psum | solution.py:29
  296.6 11.5 %psum.52 = f32[]{:T(128)} all-reduce(f32[]{:T(128)} %psum.51), channel_id=1, replica_groups=mesh['task_0'=2,'task_1'=4,'mp_0'=2,'mp_1'=8,'mp_2'=2] {'task_1'}, use_global_device_ids=true, to_apply=%region_7.0 | all-reduce | flops 1 | bytes 8 | tf_op jit(solution)/shard_map/psum | solution.py:29
  308.1 5.5 %psum.53 = f32[]{:T(128)} all-reduce(f32[]{:T(128)} %psum.52), channel_id=1, replica_groups=mesh['task_0'=2,'task_1'=4,'mp_0'=2,'mp_1'=8,'mp_2'=2] {'mp_0'}, use_global_device_ids=true, to_apply=%region_8.0 | all-reduce | flops 1 | bytes 8 | tf_op jit(solution)/shard_map/psum | solution.py:29
  313.6 15.9 %psum.54 = f32[]{:T(128)} all-reduce(f32[]{:T(128)} %psum.53), channel_id=1, replica_groups=mesh['task_0'=2,'task_1'=4,'mp_0'=2,'mp_1'=8,'mp_2'=2] {'mp_1'}, use_global_device_ids=true, to_apply=%region_9.0 | all-reduce | flops 1 | bytes 8 | tf_op jit(solution)/shard_map/psum | solution.py:29
  329.5 3.1 psum.55
  332.5 50.5 %all-reduce.3.cloned.1.call-done = f32[256,1024]{1,0:T(8,128)} async-done(((f32[256,1024]{1,0:T(8,128)}), f32[256,1024]{1,0:T(8,128)}) %all-reduce.3.cloned.1.call-update) | async-done | bytes 1048592 | tf_op jit(solution)/shard_map/psum | solution.py:88
  383.0 2.4 fusion.3
  (25 shorter events, 2.0 us)
Async XLA Ops:
  7.2 3.1 copy-start.1
  10.2 11.6 %copy-start = (bf16[1,256,1024]{2,1,0:T(8,128)(2,1)S(1)}, bf16[1,256,1024]{2,1,0:T(8,128)(2,1)}, u32[]{:S(2)}) copy-start(bf16[1,256,1024]{2,1,0:T(8,128)(2,1)} %param.8) | copy-start | bytes 1572868
  12.1 92.9 %all-to-all-start = ((bf16[64,32,256]{2,0,1:T(8,128)(2,1)}), bf16[64,32,256]{2,0,1:T(8,128)(2,1)S(1)}, u32[]{:S(2)}, u32[]{:S(2)}) async-start(bf16[64,32,256]{2,0,1:T(8,128)(2,1)} %copy.11), calls=%async_computation | async-start | bytes 2097152 | tf_op jit(solution)/shard_map/all_to_all | solution.py:60
  21.8 109.8 %reduce-scatter.3.cloned.1.call-start = ((), (), s32[]{:S(2)}) async-start(), calls=%async_computation.3 | async-start | bytes 12582912 | tf_op jit(solution)/shard_map/reduce_scatter | solution.py:23
  111.7 20.7 %copy-start.2 = (s32[1,64]{1,0:T(1,128)S(1)}, s32[1,64]{1,0:T(1,128)}, u32[]{:S(2)}) copy-start(s32[1,64]{1,0:T(1,128)} %param.11) | copy-start | bytes 772
  111.7 102.6 %reduce-scatter.5.cloned.1.call-start = ((), (), s32[]{:S(2)}) async-start(), calls=%async_computation.4 | async-start | bytes 4456448 | tf_op jit(solution)/shard_map/reduce_scatter | solution.py:24
  131.6 153.0 %all-gather.2.cloned.1.call-start = ((), (), s32[]{:S(2)}) async-start(), calls=%async_computation.5 | async-start | bytes 4325376 | tf_op jit(solution)/shard_map/all_gather | solution.py:84
  220.2 162.8 %all-reduce.3.cloned.1.call-start = ((), (), s32[]{:S(2)}) async-start(), calls=%async_computation.6 | async-start | bytes 2097152 | tf_op jit(solution)/shard_map/psum | solution.py:88
Sparse Core Ops, SparseCore 0:
  111.8 19.7 reduce-scatter.2
  134.1 80.0 reduce-scatter.4
  220.3 64.1 all-gather.1
  289.1 93.8 all-reduce.2
where the time goes:
time: 392 us
  waiting for transfers between devices  216 us (55%)
  blocking collectives  125 us (32%)
  between operations  15.3 us (4%)
  starting transfers between devices  9.82 us (3%)
  other arithmetic  9.5 us (2%)
  local copies, waits for them, and re-layouts  9.36 us (2%)
  matrix products  6.95 us (2%)
    psum x1, blocking collectives, local(): mixed = lax.psum(coeff[0] * tau_local, TASK)  81.8 us
    reduce_scatter x1, waiting for transfers between devices, scatter_pairs(): return lax.psum_scatter(tiles, chips, scatter_dimension=0, tiled=True)[0]  81.7 us
    all_gather x1, waiting for transfers between devices, local(): lax.all_gather(back, MP, axis=0, tiled=True)  64.3 us
    psum x1, waiting for transfers between devices, local(): wgrad = lax.psum(local_grad, TASK)  50.5 us
    psum x5, blocking collectives, by_axis(): value = lax.psum(value, axis)  42.9 us
    reduce_scatter x1, waiting for transfers between devices, scatter_pairs(): tiles = lax.psum_scatter(tiles, core, scatter_dimension=0, tiled=True)  19.8 us
    all_to_all x1, starting transfers between devices, local(): lax.all_to_all(normed, MP, split_axis=1, concat_axis=0, tiled=True)  9.65 us
  transfers between devices with their start and end apart: 5, of which 4 were waited for; matrix products, arithmetic and copies ran while one was open for 0% of the time, Pallas kernels for 0%

commit v1 on v0

--- a/solution.py
+++ b/solution.py
@@ -81,7 +81,7 @@
     block = columns
     local_grad = lax.dot_general(
         block,
-        lax.all_gather(back, MP, axis=0, tiled=True),
+        jnp.concatenate(lax.all_to_all(jnp.stack([back] * lax.axis_size(MP)), MP, 0, 0), axis=0),
         (((0,), (0,)), ((), ())),
         preferred_element_type=jnp.float32,
     )

time: 392 us -> 424 us (1.082)
  blocking collectives: 125 us -> 225 us
  waiting for transfers between devices: 216 us -> 150 us
    all_to_all x0 -> x1, blocking collectives: none -> 103 us  [local(): lax.all_to_all(jnp.stack([back] * lax.axis_size(MP)), MP, 0, 0)]
    all_gather x1 -> x0, waiting for transfers between devices: 64.3 us -> none  [local(): lax.all_gather(back, MP, axis=0, tiled=True)]
  transfers between devices with their start and end apart: 5 -> 4, of which waited for: 4 -> 3; matrix products, arithmetic and copies ran while one was open for 0% -> 0% of each run, Pallas kernels for 0% -> 0%
where the time goes in v1:
time: 424 us
  blocking collectives  225 us (53%)
  waiting for transfers between devices  150 us (35%)
  between operations  15.3 us (4%)
  other arithmetic  11.5 us (3%)
  starting transfers between devices  9.78 us (2%)
  local copies, waits for them, and re-layouts  7.71 us (2%)
  matrix products  4.76 us (1%)
    all_to_all x1, blocking collectives, local(): lax.all_to_all(jnp.stack([back] * lax.axis_size(MP)), MP, 0, 0)  103 us
    psum x1, blocking collectives, local(): mixed = lax.psum(coeff[0] * tau_local, TASK)  81.8 us
    reduce_scatter x1, waiting for transfers between devices, scatter_pairs(): return lax.psum_scatter(tiles, chips, scatter_dimension=0, tiled=True)[0]  81.7 us
    psum x1, waiting for transfers between devices, local(): wgrad = lax.psum(local_grad, TASK)  48.3 us
    psum x5, blocking collectives, by_axis(): value = lax.psum(value, axis)  40.8 us
    reduce_scatter x1, waiting for transfers between devices, scatter_pairs(): tiles = lax.psum_scatter(tiles, core, scatter_dimension=0, tiled=True)  19.8 us
    all_to_all x1, starting transfers between devices, local(): lax.all_to_all(normed, MP, split_axis=1, concat_axis=0, tiled=True)  9.66 us
  transfers between devices with their start and end apart: 4, of which 3 were waited for; matrix products, arithmetic and copies ran while one was open for 0% of the time, Pallas kernels for 0%

profile of v1, /device:TPU:32, one launch (start us, length us, event | category | flops | bytes accessed | tf_op | source)
XLA Modules:
  0.0 423.9 jit_solution(17464864771849105129)
XLA Ops:
  7.2 1.5 multiply_reduce_fusion
  8.7 1.6 copy.10
  10.3 2.2 fusion.1
  12.6 9.7 %all-to-all-start = ((bf16[64,32,256]{2,0,1:T(8,128)(2,1)}), bf16[64,32,256]{2,0,1:T(8,128)(2,1)S(1)}, u32[]{:S(2)}, u32[]{:S(2)}) async-start(bf16[64,32,256]{2,0,1:T(8,128)(2,1)} %fusion.1), calls=%async_computation | async-start | bytes 2097152 | tf_op jit(solution)/shard_map/all_to_all | solution.py:60
  22.3 1.4 convert_multiply_fusion
  23.6 81.8 %all-reduce.4 = bf16[256,1024]{1,0:T(8,128)(2,1)S(1)} all-reduce(f32[256,1024]{1,0:T(8,128)S(1)} %convert_multiply_fusion), channel_id=1, replica_groups=mesh['task_0'=2,'task_1'=4,'mp_0'=2,'mp_1'=8,'mp_2'=2] {'task_0','task_1'}, use_global_device_ids=true, to_apply=%region_1.0 | all-reduce | flops 262144 | bytes 1572864 | tf_op jit(solution)/shard_map/psum | solution.py:62
  105.5 1.3 fusion.9
  106.7 1.3 convolution_subtract_fusion
  108.0 4.1 copy.9
  112.2 19.8 %reduce-scatter.3.cloned.1.call-done = f32[16,64,1024]{2,1,0:T(8,128)} async-done(((f32[32,64,1024]{2,1,0:T(8,128)}), f32[16,64,1024]{2,1,0:T(8,128)}) %reduce-scatter.3.cloned.1.call-update) | async-done | bytes 4194320 | tf_op jit(solution)/shard_map/reduce_scatter | solution.py:23
  133.0 81.7 %reduce-scatter.5.cloned.1.call-done = f32[1,64,1024]{2,1,0:T(8,128)} async-done(((f32[16,64,1024]{2,1,0:T(8,128)}), f32[1,64,1024]{2,1,0:T(8,128)}) %reduce-scatter.5.cloned.1.call-update) | async-done | bytes 262160 | tf_op jit(solution)/shard_map/reduce_scatter | solution.py:24
  214.7 1.3 reshape_squeeze.3
  216.6 1.8 fusion.5
  218.4 0.7 subtract_convert_fusion
  219.1 0.7 pad_maximum_fusion.1
  220.5 102.5 %all_to_all.21 = bf16[32,64,1024]{2,1,0:T(8,128)(2,1)S(1)} all-to-all(bf16[32,64,1024]{2,1,0:T(8,128)(2,1)S(1)} %stack.9), channel_id=1, replica_groups=mesh['task_0'=2,'task_1'=4,'mp_0'=2,'mp_1'=8,'mp_2'=2] {'mp_0','mp_1','m..., dimensions={0} | all-to-all | bytes 8388608 | tf_op jit(solution)/shard_map/all_to_all | solution.py:84
  323.0 2.3 convolution_bitcast_fusion
  325.9 6.9 %psum.51 = f32[]{:T(128)} all-reduce(f32[]{:T(128)S(6)} %mul.221), channel_id=1, replica_groups=mesh['task_0'=2,'task_1'=4,'mp_0'=2,'mp_1'=8,'mp_2'=2] {'task_0'}, use_global_device_ids=true, to_apply=%region_6.0 | all-reduce | flops 1 | bytes 8 | tf_op jit(solution)/shard_map/psum | solution.py:29
  332.9 10.8 %psum.52 = f32[]{:T(128)} all-reduce(f32[]{:T(128)} %psum.51), channel_id=1, replica_groups=mesh['task_0'=2,'task_1'=4,'mp_0'=2,'mp_1'=8,'mp_2'=2] {'task_1'}, use_global_device_ids=true, to_apply=%region_7.0 | all-reduce | flops 1 | bytes 8 | tf_op jit(solution)/shard_map/psum | solution.py:29
  343.7 5.5 %psum.53 = f32[]{:T(128)} all-reduce(f32[]{:T(128)} %psum.52), channel_id=1, replica_groups=mesh['task_0'=2,'task_1'=4,'mp_0'=2,'mp_1'=8,'mp_2'=2] {'mp_0'}, use_global_device_ids=true, to_apply=%region_8.0 | all-reduce | flops 1 | bytes 8 | tf_op jit(solution)/shard_map/psum | solution.py:29
  349.2 14.4 %psum.54 = f32[]{:T(128)} all-reduce(f32[]{:T(128)} %psum.53), channel_id=1, replica_groups=mesh['task_0'=2,'task_1'=4,'mp_0'=2,'mp_1'=8,'mp_2'=2] {'mp_1'}, use_global_device_ids=true, to_apply=%region_9.0 | all-reduce | flops 1 | bytes 8 | tf_op jit(solution)/shard_map/psum | solution.py:29
  363.6 3.1 psum.55
  366.7 48.3 %all-reduce.3.cloned.1.call-done = f32[256,1024]{1,0:T(8,128)} async-done(((f32[256,1024]{1,0:T(8,128)}), f32[256,1024]{1,0:T(8,128)}) %all-reduce.3.cloned.1.call-update) | async-done | bytes 1048592 | tf_op jit(solution)/shard_map/psum | solution.py:88
  415.0 2.4 fusion.3
  (23 shorter events, 1.7 us)
Async XLA Ops:
  7.2 3.1 copy-start.1
  8.7 13.6 %copy-start = (bf16[1,256,1024]{2,1,0:T(8,128)(2,1)S(1)}, bf16[1,256,1024]{2,1,0:T(8,128)(2,1)}, u32[]{:S(2)}) copy-start(bf16[1,256,1024]{2,1,0:T(8,128)(2,1)} %param.8) | copy-start | bytes 1572868
  12.6 92.9 %all-to-all-start = ((bf16[64,32,256]{2,0,1:T(8,128)(2,1)}), bf16[64,32,256]{2,0,1:T(8,128)(2,1)S(1)}, u32[]{:S(2)}, u32[]{:S(2)}) async-start(bf16[64,32,256]{2,0,1:T(8,128)(2,1)} %fusion.1), calls=%async_computation | async-start | bytes 2097152 | tf_op jit(solution)/shard_map/all_to_all | solution.py:60
  22.2 109.8 %reduce-scatter.3.cloned.1.call-start = ((), (), s32[]{:S(2)}) async-start(), calls=%async_computation.4 | async-start | bytes 12582912 | tf_op jit(solution)/shard_map/reduce_scatter | solution.py:23
  112.1 20.7 %copy-start.2 = (s32[1,64]{1,0:T(1,128)S(1)}, s32[1,64]{1,0:T(1,128)}, u32[]{:S(2)}) copy-start(s32[1,64]{1,0:T(1,128)} %param.11) | copy-start | bytes 772
  112.1 102.6 %reduce-scatter.5.cloned.1.call-start = ((), (), s32[]{:S(2)}) async-start(), calls=%async_computation.5 | async-start | bytes 4456448 | tf_op jit(solution)/shard_map/reduce_scatter | solution.py:24
  132.0 283.0 %all-reduce.3.cloned.1.call-start = ((), (), s32[]{:S(2)}) async-start(), calls=%async_computation.6 | async-start | bytes 2097152 | tf_op jit(solution)/shard_map/psum | solution.py:88
Sparse Core Ops, SparseCore 0:
  112.2 19.7 reduce-scatter.2
  134.5 80.0 reduce-scatter.4
  325.4 89.5 all-reduce.2
